TPU v7x, 128 devices: a whole 4x4x4 slice. The times are simulated.
128 devices in a mesh: rack: 64 (over y, z, x_hi, core), queue: 2 (over x_lo).
Axes of the slice: x: 4 (x_hi: 2, x_lo: 2; x = x_hi * 2 + x_lo), y: 4, z: 4, core: 2. Of those that a mesh axis runs over, the one named last changes fastest.
Arguments:
- state: float32 [4096, 4096], P('rack', 'queue'), may hold values from -6 to 6
- queue_blocks: float32 [16, 3, 256, 256], P('queue'), may hold values from -0.21875 to 0.21875
- queue_rows: int32 [16, 3], P('queue'), may hold values from 0 to 15, as said below
- kill_blocks: float32 [16, 3, 256, 256], P('queue'), may hold values from -0.21875 to 0.21875
- kill_rows: int32 [16, 3], P('queue'), may hold values from 0 to 15, as said below
- rate_index: int32 [12], replicated, may hold values from 0 to 7
- rate_table: float32 [8, 2], replicated, may hold values from 0.1 to 2
Outputs:
- advanced: float32 [4096, 4096], P('rack', 'queue')
Inputs may be any that keep to these rules, and one draw needn't show every extreme that they name: `queue_rows`: column block c's first row block is c, and its three row blocks are distinct. `kill_rows`: column block c's first row block is c, and its three row blocks are distinct.
All inputs are finite; a program needn't handle non-finite values.
Results may differ from a plain program's by a relative error of at most 0.0001.
Values sent between devices are 32-bit elements; how exact they have to be, the bound alone decides.
A program may use at most 128 MiB of HBM per device.

v0:
```python
import jax
import jax.numpy as jnp
from jax import lax
from jax.sharding import PartitionSpec as P

STEPS = 2


def from_partner(value, axis, stride):
    mask = 2**stride
    pairs = [(source, source ^ mask) for source in range(lax.axis_size(axis))]
    return lax.ppermute(value, axis, pairs)


def apply_blocks(whole, blocks, rows):
    patterns = whole.shape[0]
    pieces = whole.reshape(patterns, -1, blocks.shape[2])
    chosen = jnp.take(pieces, rows, axis=1)
    result = jnp.einsum(
        "pcjt,cjts->pcs",
        chosen,
        blocks,
        precision=lax.Precision.HIGHEST,
        preferred_element_type=jnp.float32,
    )
    return result.reshape(patterns, -1)


def bit_terms(current, killed, fail, repair, first, count):
    total = jnp.zeros_like(current)
    rows = current.shape[0]
    for bit in range(count):
        shape = (rows // 2 ** (bit + 1), 2, 2**bit) + current.shape[1:]
        upper = current.reshape(shape)
        lower = killed.reshape(shape)
        term = jnp.stack(
            (repair[first + bit] * upper[:, 1], fail[first + bit] * lower[:, 0]), axis=1
        )
        total = total + term.reshape(current.shape)
    return total


def local(state, queue_blocks, queue_rows, kill_blocks, kill_rows, rate_index, rate_table):
    fail = rate_table[rate_index, 0]
    repair = rate_table[rate_index, 1]
    scale_sum = 1.0 + jnp.sum(fail + repair)
    patterns = state.shape[0]
    low_count = patterns.bit_length() - 1
    high_count = lax.axis_size("rack").bit_length() - 1
    rack_place = lax.axis_index("rack")
    pattern = lax.broadcasted_iota(jnp.int32, (patterns, 1), 0)
    leaving = jnp.zeros((patterns, 1), jnp.float32)
    for bit in range(low_count):
        flag = pattern // 2**bit % 2
        leaving = leaving + jnp.where(flag == 1, repair[bit], fail[bit])
    for bit in range(high_count):
        flag = rack_place // 2**bit % 2
        leaving = leaving + jnp.where(flag == 1, repair[low_count + bit], fail[low_count + bit])
    current = state
    for step in range(STEPS):
        whole = lax.all_gather(current, "queue", axis=1, tiled=True)
        queue_part = apply_blocks(whole, queue_blocks, queue_rows)
        killed = apply_blocks(whole, kill_blocks, kill_rows)
        rack_part = bit_terms(current, killed, fail, repair, 0, low_count)
        order = range(high_count)
        for bit in order:
            flag = rack_place // 2**bit % 2
            outgoing = jnp.where(flag == 1, current, killed)
            incoming = from_partner(outgoing, "rack", bit)
            rack_part = (
                rack_part
                + jnp.where(flag == 1, fail[low_count + bit], repair[low_count + bit]) * incoming
            )
        current = current + (queue_part + rack_part - leaving * current) / scale_sum
    return current


def solution(mesh):
    placed = (
        P("rack", "queue"),
        P("queue", None, None, None),
        P("queue", None),
        P("queue", None, None, None),
        P("queue", None),
        P(),
        P(),
    )
    return jax.shard_map(
        local, mesh=mesh, in_specs=placed, out_specs=P("rack", "queue"), check_vma=False
    )
```

profile of v0, /device:TPU:0, one launch (start us, length us, event | category | flops | bytes accessed | tf_op | source)
XLA Modules:
  0.0 198.4 jit_solution(13551869775011367674)
XLA Ops:
  10.1 1.2 reshape.448
  15.0 1.3 slice_multiply_fusion.13
  16.4 1.3 slice_multiply_fusion.15
  18.4 1.3 slice_multiply_fusion.19
  27.2 7.4 %add_add_fusion = f32[64]{0:T(128)S(1)} fusion(f32[]{:T(128)S(6)} %select_n.398, f32[]{:T(128)S(6)} %select_n.397, f32[]{:T(128)S(6)} %select_n.396, f32[]{:T(128)S(6)} %select_n.395, f32[]{:T(128)S(6)} %select_n.394, f32[]{:T(128)S(6)} %select_n.393, f32[]{:T(128)} %bitcast.27, f32[]{:T(128)} %bitcast.25, f32[]{:T(128)} %bitcast.23, f32[]{:T(128)} %bitcast.21, ...), kind=kLoop, calls=%fused_computation.162 | loop fusion | flops 7296 | bytes 328 | tf_op jit(solution)/shard_map/add | solution.py:58
  43.7 1.5 slice_multiply_fusion.21
  45.2 1.6 slice_multiply_fusion.23
  46.8 1.3 copy.85
  48.1 1.8 gather_fusion.3
  49.9 7.3 %fusion.4 = f32[8,64,256,1]{2,1,3,0:T(8,128)S(1)} fusion(f32[8,3,256,256]{3,2,1,0:T(8,128)} %param.12, f32[8,3,64,256]{3,2,1,0:T(8,128)} %bitcast.165, pred[8,3]{1,0:T(8,128)(4,1)S(1)} %copy.48), kind=kOutput, calls=%fused_computation.10 | convolution fusion | flops 1208352768 | bytes 8388632 | tf_op jit(solution)/shard_map/pcjt,cjts->pcs/dot_general | solution.py:19
  57.5 0.9 reshape_reshape.41
  58.4 0.9 reshape_reshape.40
  59.3 0.9 reshape_reshape.39
  60.2 1.0 reshape_reshape.38
  61.5 1.8 gather_fusion.2
  63.4 1.7 slice_multiply_fusion.12
  65.0 2.3 %slice_multiply_fusion.14 = f32[2,1,16,2048]{3,2,1,0:T(8,128)} fusion(f32[2,2,16,2048]{3,2,1,0:T(8,128)} %reshape_reshape.40, f32[]{:T(128)} %bitcast.23), kind=kLoop, calls=%fused_computation.82 | loop fusion | flops 65536 | bytes 524292 | tf_op jit(solution)/shard_map/mul | solution.py:37
  67.3 2.4 %slice_multiply_fusion.16 = f32[4,1,8,2048]{3,2,1,0:T(8,128)} fusion(f32[4,2,8,2048]{3,2,1,0:T(8,128)} %reshape_reshape.39, f32[]{:T(128)} %bitcast.19), kind=kLoop, calls=%fused_computation.84 | loop fusion | flops 65536 | bytes 524292 | tf_op jit(solution)/shard_map/mul | solution.py:37
  69.7 1.8 broadcast_select_fusion.11
  71.5 3.3 %collective-permute-start.5 = (f32[64,2048]{1,0:T(8,128)}, f32[64,2048]{1,0:T(8,128)}, u32[]{:S(2)}, u32[]{:S(2)}) collective-permute-start(f32[64,2048]{1,0:T(8,128)} %get-tuple-element.19), channel_id=1, source_target_pairs={{0,64},{2,66},{4,68},{6,70},{8,72},{10,74},{12,76},{14,78},{16,80}... | collective-permute-start | bytes 1572872 | tf_op jit(solution)/shard_map/ppermute | solution.py:12
  75.5 3.9 %collective-permute-start.3 = (f32[64,2048]{1,0:T(8,128)}, f32[64,2048]{1,0:T(8,128)}, u32[]{:S(2)}, u32[]{:S(2)}) collective-permute-start(f32[64,2048]{1,0:T(8,128)} %get-tuple-element.16), channel_id=1, source_target_pairs={{0,16},{2,18},{4,20},{6,22},{8,24},{10,26},{12,28},{14,30},{16,0},... | collective-permute-start | bytes 1572872 | tf_op jit(solution)/shard_map/ppermute | solution.py:12
  79.4 1.0 collective-permute-start.2
  80.4 3.0 %collective-permute-start.1 = (f32[64,2048]{1,0:T(8,128)}, f32[64,2048]{1,0:T(8,128)}, u32[]{:S(2)}, u32[]{:S(2)}) collective-permute-start(f32[64,2048]{1,0:T(8,128)} %get-tuple-element.18), channel_id=1, source_target_pairs={{0,4},{2,6},{4,0},{6,2},{8,12},{10,14},{12,8},{14,10},{16,20},{18,... | collective-permute-start | bytes 1572872 | tf_op jit(solution)/shard_map/ppermute | solution.py:12
  85.2 6.2 %fusion.12 = f32[8,8,8,256]{3,2,1,0:T(8,128)S(1)} fusion(f32[8,3,256,256]{3,2,1,0:T(8,128)} %param.10, f32[8,3,64,256]{3,2,1,0:T(8,128)S(1)} %bitcast.162, pred[8,3]{1,0:T(8,128)(4,1)S(1)} %copy.44), kind=kOutput, calls=%fused_computation.18 | convolution fusion | flops 1208352768 | bytes 8388632 | tf_op jit(solution)/shard_map/pcjt,cjts->pcs/dot_general | solution.py:19
  91.8 1.1 reshape_reshape.37
  92.9 1.6 slice_multiply_fusion.20
  94.7 2.1 %pad_maximum_fusion.1 = f32[16,2,2,2048]{3,2,1,0:T(2,128)} fusion(f32[16,1,2,2048]{3,2,1,0:T(2,128)S(1)} %slice_multiply_fusion.20, f32[16,1,2,2048]{3,2,1,0:T(2,128)} %slice_multiply_fusion.21), kind=kLoop, calls=%fused_computation.31 | loop fusion | flops 131072 | bytes 1048576 | tf_op jit(solution)/shard_map/stack | solution.py:36
  97.4 1.4 reshape.447
  98.8 1.1 pad_maximum_fusion.4
  99.9 1.0 pad_maximum_fusion.3
  100.9 2.1 %collective-permute-done.2 = f32[64,2048]{1,0:T(8,128)} collective-permute-done((f32[64,2048]{1,0:T(8,128)}, f32[64,2048]{1,0:T(8,128)}, u32[]{:S(2)}, u32[]{:S(2)}) %collective-permute-start.2) | collective-permute-done | bytes 524320 | tf_op jit(solution)/shard_map/ppermute | solution.py:12
  103.0 3.4 %fusion.45 = f32[64,2048]{1,0:T(8,128)} fusion(f32[64,2048]{1,0:T(8,128)S(1)} %copy-done.3, f32[64,2048]{1,0:T(8,128)S(1)} %bitcast.171, f32[1,2,32,2048]{3,2,1,0:T(8,128)S(1)} %pad_maximum_fusion.5, f32[2,2,16,2048]{3,2,1,0:T(8,128)S(1)} %pad_maximum_fusion.4, f32[4,2,8,2048]{3,2,1,0:T(8,128)S(1)} %pad_maximum_fusion.3, ...), kind=kLoop, calls=%fused_computation.65 | loop fusion | flops 2883584 | bytes 7864604 | tf_op jit(solution)/shard_map/add | solution.py:74
  106.4 1.2 reshape.463
  107.7 1.3 slice_multiply_fusion.1
  109.0 1.3 slice_multiply_fusion.3
  111.0 1.3 slice_multiply_fusion.7
  112.9 1.4 slice_multiply_fusion.9
  114.4 1.6 slice_multiply_fusion.11
  116.0 12.6 %all-gather.5.cloned.1.call-done = f32[64,4096]{1,0:T(8,128)} async-done(((f32[64,2048]{1,0:T(8,128)}), f32[64,4096]{1,0:T(8,128)}) %all-gather.5.cloned.1.call-update) | async-done | bytes 1048592 | tf_op jit(solution)/shard_map/all_gather | solution.py:61
  128.6 1.3 copy.84
  130.5 1.8 gather_fusion.5
  132.4 7.3 %fusion = f32[8,64,256,1]{2,1,3,0:T(8,128)S(1)} fusion(f32[8,3,256,256]{3,2,1,0:T(8,128)} %param.12, f32[8,3,64,256]{3,2,1,0:T(8,128)} %bitcast.164, pred[8,3]{1,0:T(8,128)(4,1)S(1)} %copy.48), kind=kOutput, calls=%fused_computation.6 | convolution fusion | flops 1208352768 | bytes 8388632 | tf_op jit(solution)/shard_map/pcjt,cjts->pcs/dot_general | solution.py:19
  140.0 0.9 reshape_reshape.47
  140.9 0.9 reshape_reshape.46
  141.7 0.9 reshape_reshape.45
  142.6 1.0 reshape_reshape.44
  143.7 1.1 reshape_reshape.42
  144.8 7.7 %fusion.15 = f32[8,8,8,256]{3,2,1,0:T(8,128)} fusion(f32[8,3,256,256]{3,2,1,0:T(8,128)} %param.10, f32[8,3,64,256]{3,2,1,0:T(8,128)S(1)} %bitcast.163, pred[8,3]{1,0:T(8,128)(4,1)S(1)} %copy.44), kind=kOutput, calls=%fused_computation.19 | convolution fusion | flops 1208352768 | bytes 8388632 | tf_op jit(solution)/shard_map/pcjt,cjts->pcs/dot_general | solution.py:19
  153.3 1.3 slice_multiply_fusion.2
  154.6 1.4 slice_multiply_fusion.4
  156.1 2.0 %broadcast_select_fusion.10 = (f32[64,2048]{1,0:T(8,128)}, f32[64,2048]{1,0:T(8,128)}, f32[64,2048]{1,0:T(8,128)}, f32[64,2048]{1,0:T(8,128)}, f32[64,2048]{1,0:T(8,128)}, /*index=5*/f32[64,2048]{1,0:T(8,128)}) fusion(f32[64,2048]{1,0:T(8,128)S(1)} %copy-done.2, f32[64,2048]{1,0:T(8,128)S(1)} %bitcast.172, pred[]{:T(512)S(6)} %eq.116, pred[]{:T(512)S(6)} %eq.121, ...), kind=kLoop, calls=%fused_computation.102 | loop fusion | flops 786432 | bytes 4194310 | tf_op jit(solution)/shard_map/jit(_where)/select_n | solution.py:68
  158.1 3.0 %collective-permute-start.11 = (f32[64,2048]{1,0:T(8,128)}, f32[64,2048]{1,0:T(8,128)}, u32[]{:S(2)}, u32[]{:S(2)}) collective-permute-start(f32[64,2048]{1,0:T(8,128)} %get-tuple-element.9), channel_id=1, source_target_pairs={{0,64},{2,66},{4,68},{6,70},{8,72},{10,74},{12,76},{14,78},{16,80}... | collective-permute-start | bytes 1572872 | tf_op jit(solution)/shard_map/ppermute | solution.py:12
  161.7 3.2 %collective-permute-start.9 = (f32[64,2048]{1,0:T(8,128)}, f32[64,2048]{1,0:T(8,128)}, u32[]{:S(2)}, u32[]{:S(2)}) collective-permute-start(f32[64,2048]{1,0:T(8,128)} %get-tuple-element.11), channel_id=1, source_target_pairs={{0,16},{2,18},{4,20},{6,22},{8,24},{10,26},{12,28},{14,30},{16,0},... | collective-permute-start | bytes 1572872 | tf_op jit(solution)/shard_map/ppermute | solution.py:12
  165.5 2.7 %collective-permute-start.7 = (f32[64,2048]{1,0:T(8,128)}, f32[64,2048]{1,0:T(8,128)}, u32[]{:S(2)}, u32[]{:S(2)}) collective-permute-start(f32[64,2048]{1,0:T(8,128)} %get-tuple-element.13), channel_id=1, source_target_pairs={{0,4},{2,6},{4,0},{6,2},{8,12},{10,14},{12,8},{14,10},{16,20},{18,... | collective-permute-start | bytes 1572872 | tf_op jit(solution)/shard_map/ppermute | solution.py:12
  170.4 1.1 reshape_reshape.43
  171.6 1.6 slice_multiply_fusion.8
  173.2 1.5 collective-permute-done.11
  174.7 2.1 %pad_maximum_fusion.7 = f32[16,2,2,2048]{3,2,1,0:T(2,128)} fusion(f32[16,1,2,2048]{3,2,1,0:T(2,128)S(1)} %slice_multiply_fusion.8, f32[16,1,2,2048]{3,2,1,0:T(2,128)} %slice_multiply_fusion.9), kind=kLoop, calls=%fused_computation.37 | loop fusion | flops 131072 | bytes 1048576 | tf_op jit(solution)/shard_map/stack | solution.py:36
  177.4 1.4 reshape.462
  178.9 1.1 pad_maximum_fusion.10
  179.9 1.0 pad_maximum_fusion.9
  181.0 3.9 %collective-permute-done.10 = f32[64,2048]{1,0:T(8,128)} collective-permute-done((f32[64,2048]{1,0:T(8,128)}, f32[64,2048]{1,0:T(8,128)}, u32[]{:S(2)}, u32[]{:S(2)}) %collective-permute-start.10) | collective-permute-done | bytes 524320 | tf_op jit(solution)/shard_map/ppermute | solution.py:12
  184.9 3.2 %collective-permute-done.8 = f32[64,2048]{1,0:T(8,128)} collective-permute-done((f32[64,2048]{1,0:T(8,128)}, f32[64,2048]{1,0:T(8,128)}, u32[]{:S(2)}, u32[]{:S(2)}) %collective-permute-start.8) | collective-permute-done | bytes 524320 | tf_op jit(solution)/shard_map/ppermute | solution.py:12
  188.1 3.4 %fusion.35 = f32[64,2048]{1,0:T(8,128)} fusion(f32[64,2048]{1,0:T(8,128)S(1)} %copy-done.2, f32[64,2048]{1,0:T(8,128)S(1)} %bitcast.170, f32[1,2,32,2048]{3,2,1,0:T(8,128)S(1)} %pad_maximum_fusion.11, f32[2,2,16,2048]{3,2,1,0:T(8,128)S(1)} %pad_maximum_fusion.10, f32[4,2,8,2048]{3,2,1,0:T(8,128)S(1)} %pad_maximum_fusion.9, ...), kind=kLoop, calls=%fused_computation.52 | loop fusion | flops 2883584 | bytes 7864604 | tf_op jit(solution)/shard_map/add | solution.py:74
  (103 shorter events, 20.2 us)
Async XLA Ops:
  6.5 4.7 %copy-start = (f32[8,2]{0,1:T(2,128)S(1)}, f32[8,2]{0,1:T(2,128)}, u32[]{:S(2)}) copy-start(f32[8,2]{0,1:T(2,128)} %param.15) | copy-start | bytes 196
  6.5 8.5 %copy-start.3 = (f32[64,2048]{1,0:T(8,128)S(1)}, f32[64,2048]{1,0:T(8,128)}, u32[]{:S(2)}) copy-start(f32[64,2048]{1,0:T(8,128)} %param.9) | copy-start | bytes 1572868
  6.5 4.7 %copy-start.18 = (s32[12]{0:T(128)S(1)}, s32[12]{0:T(128)}, u32[]{:S(2)}) copy-start(s32[12]{0:T(128)} %param.14) | copy-start | bytes 148
  6.5 40.2 %all-gather.3.cloned.1.call-start = ((), (), s32[]{:S(2)}) async-start(), calls=%async_computation | async-start | bytes 1572864 | tf_op jit(solution)/shard_map/all_gather | solution.py:61
  7.3 121.3 %all-gather.5.cloned.1.call-start = ((), (), s32[]{:S(2)}) async-start(), calls=%async_computation.1 | async-start | bytes 1572864 | tf_op jit(solution)/shard_map/all_gather | solution.py:61
  69.7 13.7 %copy-start.8 = (f32[8,2,4,2048]{3,2,1,0:T(4,128)S(1)}, f32[8,2,4,2048]{3,2,1,0:T(4,128)}, u32[]{:S(2)}) copy-start(f32[8,2,4,2048]{3,2,1,0:T(4,128)} %reshape_reshape.38) | copy-start | bytes 1572868
  69.7 15.2 %copy-start.12 = (f32[1,1,32,2048]{3,2,1,0:T(8,128)S(1)}, f32[1,1,32,2048]{3,2,1,0:T(8,128)}, u32[]{:S(2)}) copy-start(f32[1,1,32,2048]{3,2,1,0:T(8,128)} %slice_multiply_fusion.13) | copy-start | bytes 786436
  71.5 13.5 %copy-start.13 = (f32[8,1,4,2048]{3,2,1,0:T(4,128)S(1)}, f32[8,1,4,2048]{3,2,1,0:T(4,128)}, u32[]{:S(2)}) copy-start(f32[8,1,4,2048]{3,2,1,0:T(4,128)} %slice_multiply_fusion.19) | copy-start | bytes 786436
  71.5 23.0 %collective-permute-start.5 = (f32[64,2048]{1,0:T(8,128)}, f32[64,2048]{1,0:T(8,128)}, u32[]{:S(2)}, u32[]{:S(2)}) collective-permute-start(f32[64,2048]{1,0:T(8,128)} %get-tuple-element.19), channel_id=1, source_target_pairs={{0,64},{2,66},{4,68},{6,70},{8,72},{10,74},{12,76},{14,78},{16,80}... | collective-permute-start | bytes 1572872 | tf_op jit(solution)/shard_map/ppermute | solution.py:12
  74.8 26.1 %collective-permute-start.4 = (f32[64,2048]{1,0:T(8,128)}, f32[64,2048]{1,0:T(8,128)}, u32[]{:S(2)}, u32[]{:S(2)}) collective-permute-start(f32[64,2048]{1,0:T(8,128)} %get-tuple-element.15), channel_id=1, source_target_pairs={{0,32},{2,34},{4,36},{6,38},{8,40},{10,42},{12,44},{14,46},{16,48}... | collective-permute-start | bytes 1572872 | tf_op jit(solution)/shard_map/ppermute | solution.py:12
  75.5 25.4 %collective-permute-start.3 = (f32[64,2048]{1,0:T(8,128)}, f32[64,2048]{1,0:T(8,128)}, u32[]{:S(2)}, u32[]{:S(2)}) collective-permute-start(f32[64,2048]{1,0:T(8,128)} %get-tuple-element.16), channel_id=1, source_target_pairs={{0,16},{2,18},{4,20},{6,22},{8,24},{10,26},{12,28},{14,30},{16,0},... | collective-permute-start | bytes 1572872 | tf_op jit(solution)/shard_map/ppermute | solution.py:12
  79.4 23.6 %collective-permute-start.2 = (f32[64,2048]{1,0:T(8,128)}, f32[64,2048]{1,0:T(8,128)}, u32[]{:S(2)}, u32[]{:S(2)}) collective-permute-start(f32[64,2048]{1,0:T(8,128)} %get-tuple-element.17), channel_id=1, source_target_pairs={{0,8},{2,10},{4,12},{6,14},{8,0},{10,2},{12,4},{14,6},{16,24},{18,... | collective-permute-start | bytes 1572872 | tf_op jit(solution)/shard_map/ppermute | solution.py:12
  80.4 4.7 %copy-start.4 = (f32[24,64,256]{2,1,0:T(8,128)S(1)}, f32[24,64,256]{2,1,0:T(8,128)}, u32[]{:S(2)}) copy-start(f32[24,64,256]{2,1,0:T(8,128)} %gather_fusion.2) | copy-start | bytes 4718596
  80.4 22.6 %collective-permute-start.1 = (f32[64,2048]{1,0:T(8,128)}, f32[64,2048]{1,0:T(8,128)}, u32[]{:S(2)}, u32[]{:S(2)}) collective-permute-start(f32[64,2048]{1,0:T(8,128)} %get-tuple-element.18), channel_id=1, source_target_pairs={{0,4},{2,6},{4,0},{6,2},{8,12},{10,14},{12,8},{14,10},{16,20},{18,... | collective-permute-start | bytes 1572872 | tf_op jit(solution)/shard_map/ppermute | solution.py:12
  85.1 6.2 %copy-start.17 = (f32[32,1,1,2048]{3,1,0,2:T(1,128)S(1)}, f32[32,1,1,2048]{3,1,0,2:T(1,128)}, u32[]{:S(2)}) copy-start(f32[32,1,1,2048]{3,1,0,2:T(1,128)} %slice_multiply_fusion.23) | copy-start | bytes 786436
  94.6 8.4 %collective-permute-start = (f32[64,2048]{1,0:T(8,128)}, f32[64,2048]{1,0:T(8,128)}, u32[]{:S(2)}, u32[]{:S(2)}) collective-permute-start(f32[64,2048]{1,0:T(8,128)} %get-tuple-element.14), channel_id=1, source_target_pairs={{0,2},{2,0},{4,6},{6,4},{8,10},{10,8},{12,14},{14,12},{16,18},{18,... | collective-permute-start | bytes 1572872 | tf_op jit(solution)/shard_map/ppermute | solution.py:12
  106.4 1.3 copy-start.2
  144.8 7.7 %copy-start.11 = (f32[1,2,32,2048]{3,2,1,0:T(8,128)S(1)}, f32[1,2,32,2048]{3,2,1,0:T(8,128)}, u32[]{:S(2)}) copy-start(f32[1,2,32,2048]{3,2,1,0:T(8,128)} %reshape_reshape.47) | copy-start | bytes 1572868
  144.8 8.5 %copy-start.10 = (f32[2,2,16,2048]{3,2,1,0:T(8,128)S(1)}, f32[2,2,16,2048]{3,2,1,0:T(8,128)}, u32[]{:S(2)}) copy-start(f32[2,2,16,2048]{3,2,1,0:T(8,128)} %reshape_reshape.46) | copy-start | bytes 1572868
  144.8 9.8 %copy-start.9 = (f32[4,2,8,2048]{3,2,1,0:T(8,128)S(1)}, f32[4,2,8,2048]{3,2,1,0:T(8,128)}, u32[]{:S(2)}) copy-start(f32[4,2,8,2048]{3,2,1,0:T(8,128)} %reshape_reshape.45) | copy-start | bytes 1572868
  156.0 12.1 %copy-start.7 = (f32[8,2,4,2048]{3,2,1,0:T(4,128)S(1)}, f32[8,2,4,2048]{3,2,1,0:T(4,128)}, u32[]{:S(2)}) copy-start(f32[8,2,4,2048]{3,2,1,0:T(4,128)} %reshape_reshape.44) | copy-start | bytes 1572868
  156.0 12.8 %copy-start.6 = (f32[32,2,1,2048]{3,1,0,2:T(2,128)S(1)}, f32[32,2,1,2048]{3,1,0,2:T(2,128)}, u32[]{:S(2)}) copy-start(f32[32,2,1,2048]{3,1,0,2:T(2,128)} %reshape_reshape.42) | copy-start | bytes 1572868
  156.1 13.6 %copy-start.14 = (f32[1,1,32,2048]{3,2,1,0:T(8,128)S(1)}, f32[1,1,32,2048]{3,2,1,0:T(8,128)}, u32[]{:S(2)}) copy-start(f32[1,1,32,2048]{3,2,1,0:T(8,128)} %slice_multiply_fusion.1) | copy-start | bytes 786436
  158.1 11.7 %copy-start.15 = (f32[8,1,4,2048]{3,2,1,0:T(4,128)S(1)}, f32[8,1,4,2048]{3,2,1,0:T(4,128)}, u32[]{:S(2)}) copy-start(f32[8,1,4,2048]{3,2,1,0:T(4,128)} %slice_multiply_fusion.7) | copy-start | bytes 786436
  158.1 16.6 %collective-permute-start.11 = (f32[64,2048]{1,0:T(8,128)}, f32[64,2048]{1,0:T(8,128)}, u32[]{:S(2)}, u32[]{:S(2)}) collective-permute-start(f32[64,2048]{1,0:T(8,128)} %get-tuple-element.9), channel_id=1, source_target_pairs={{0,64},{2,66},{4,68},{6,70},{8,72},{10,74},{12,76},{14,78},{16,80}... | collective-permute-start | bytes 1572872 | tf_op jit(solution)/shard_map/ppermute | solution.py:12
  161.1 23.8 %collective-permute-start.10 = (f32[64,2048]{1,0:T(8,128)}, f32[64,2048]{1,0:T(8,128)}, u32[]{:S(2)}, u32[]{:S(2)}) collective-permute-start(f32[64,2048]{1,0:T(8,128)} %get-tuple-element.10), channel_id=1, source_target_pairs={{0,32},{2,34},{4,36},{6,38},{8,40},{10,42},{12,44},{14,46},{16,48}... | collective-permute-start | bytes 1572872 | tf_op jit(solution)/shard_map/ppermute | solution.py:12
  161.7 23.2 %collective-permute-start.9 = (f32[64,2048]{1,0:T(8,128)}, f32[64,2048]{1,0:T(8,128)}, u32[]{:S(2)}, u32[]{:S(2)}) collective-permute-start(f32[64,2048]{1,0:T(8,128)} %get-tuple-element.11), channel_id=1, source_target_pairs={{0,16},{2,18},{4,20},{6,22},{8,24},{10,26},{12,28},{14,30},{16,0},... | collective-permute-start | bytes 1572872 | tf_op jit(solution)/shard_map/ppermute | solution.py:12
  164.8 23.3 %collective-permute-start.8 = (f32[64,2048]{1,0:T(8,128)}, f32[64,2048]{1,0:T(8,128)}, u32[]{:S(2)}, u32[]{:S(2)}) collective-permute-start(f32[64,2048]{1,0:T(8,128)} %get-tuple-element.12), channel_id=1, source_target_pairs={{0,8},{2,10},{4,12},{6,14},{8,0},{10,2},{12,4},{14,6},{16,24},{18,... | collective-permute-start | bytes 1572872 | tf_op jit(solution)/shard_map/ppermute | solution.py:12
  165.5 4.4 %copy-start.16 = (f32[32,1,1,2048]{3,1,0,2:T(1,128)S(1)}, f32[32,1,1,2048]{3,1,0,2:T(1,128)}, u32[]{:S(2)}) copy-start(f32[32,1,1,2048]{3,1,0,2:T(1,128)} %slice_multiply_fusion.11) | copy-start | bytes 786436
  165.5 22.6 %collective-permute-start.7 = (f32[64,2048]{1,0:T(8,128)}, f32[64,2048]{1,0:T(8,128)}, u32[]{:S(2)}, u32[]{:S(2)}) collective-permute-start(f32[64,2048]{1,0:T(8,128)} %get-tuple-element.13), channel_id=1, source_target_pairs={{0,4},{2,6},{4,0},{6,2},{8,12},{10,14},{12,8},{14,10},{16,20},{18,... | collective-permute-start | bytes 1572872 | tf_op jit(solution)/shard_map/ppermute | solution.py:12
  170.4 6.4 %copy-start.5 = (f32[8,8,8,256]{3,2,1,0:T(8,128)S(1)}, f32[8,8,8,256]{3,2,1,0:T(8,128)}, u32[]{:S(2)}) copy-start(f32[8,8,8,256]{3,2,1,0:T(8,128)} %fusion.15) | copy-start | bytes 1572868
  174.7 13.4 %collective-permute-start.6 = (f32[64,2048]{1,0:T(8,128)}, f32[64,2048]{1,0:T(8,128)}, u32[]{:S(2)}, u32[]{:S(2)}) collective-permute-start(f32[64,2048]{1,0:T(8,128)} %get-tuple-element.8), channel_id=1, source_target_pairs={{0,2},{2,0},{4,6},{6,4},{8,10},{10,8},{12,14},{14,12},{16,18},{18,... | collective-permute-start | bytes 1572872 | tf_op jit(solution)/shard_map/ppermute | solution.py:12
  188.1 3.4 %copy-start.1 = (f32[8,2]{0,1:T(2,128)S(1)}, f32[8,2]{0,1:T(2,128)}, u32[]{:S(2)}) copy-start(f32[8,2]{0,1:T(2,128)} %param.15) | copy-start | bytes 196
Sparse Core Ops, SparseCore 0:
  9.0 26.2 all-gather.2
  106.6 21.9 all-gather.4
where the time goes:
time: 200 us; the launch traced here: 198 us
  other arithmetic  62.4 us (31%)
  local copies, waits for them, and re-layouts  31.7 us (16%)
  between operations  29.6 us (15%)
  matrix products  28.4 us (14%)
  waiting for transfers between devices  24.1 us (12%)
  starting transfers between devices  22.1 us (11%)
    dot_general x4, matrix products, apply_blocks(): jnp.einsum('pcjt,cjts->pcs', chosen, blocks, precision=lax.Precision.HIGH...  28.4 us
    ppermute x12, starting transfers between devices, from_partner(): return lax.ppermute(value, axis, pairs)  22.1 us
    mul x12, other arithmetic, bit_terms(): fail[first + bit] * lower[:, 0]  16 us
    mul x12, other arithmetic, bit_terms(): repair[first + bit] * upper[:, 1]  15.3 us
    all_gather x2, waiting for transfers between devices, local(): whole = lax.all_gather(current, 'queue', axis=1, tiled=True)  12.6 us
    another operation x12, local copies, waits for them, and re-layouts, bit_terms(): lower = killed.reshape(shape)  11 us
    ppermute x12, waiting for transfers between devices, from_partner(): return lax.ppermute(value, axis, pairs)  10.8 us
    another operation x12, other arithmetic, bit_terms(): jnp.stack((repair[first + bit] * upper[:, 1], fail[first + bit] * lower[:...  9.75 us
  transfers between devices with their start and end apart: 14, of which 5 were waited for; matrix products, arithmetic and copies ran while one was open for 31% of the time, Pallas kernels for 0%

commit v1 on v0

--- a/solution.py
+++ b/solution.py
@@ -4,6 +4,13 @@
 from jax.sharding import PartitionSpec as P
 
 STEPS = 2
+
+
+def gather_over(x, name, dim):
+    devices = lax.axis_size(name)
+    blocks = jnp.stack([x for _ in range(devices)])
+    blocks = lax.all_to_all(blocks, name, split_axis=0, concat_axis=0)
+    return jnp.concatenate(blocks, axis=dim)
 
 
 def from_partner(value, axis, stride):
@@ -58,7 +65,7 @@
         leaving = leaving + jnp.where(flag == 1, repair[low_count + bit], fail[low_count + bit])
     current = state
     for step in range(STEPS):
-        whole = lax.all_gather(current, "queue", axis=1, tiled=True)
+        whole = gather_over(current, "queue", 1)
         queue_part = apply_blocks(whole, queue_blocks, queue_rows)
         killed = apply_blocks(whole, kill_blocks, kill_rows)
         rack_part = bit_terms(current, killed, fail, repair, 0, low_count)

time: 200 us -> 184 us (0.920)
  between operations: 29.6 us -> 16.5 us
  waiting for transfers between devices: 24.1 us -> 13.8 us
  local copies, waits for them, and re-layouts: 31.7 us -> 37.1 us
  starting transfers between devices: 22.1 us -> 25.2 us
    all_gather x2 -> x0, waiting for transfers between devices: 12.6 us -> none  [local(): whole = lax.all_gather(current, 'queue', axis=1, tiled=True)]
    another operation x0 -> x4, local copies, waits for them, and re-layouts: none -> 7.34 us  [apply_blocks(): pieces = whole.reshape(patterns, -1, blocks.shape[2])]
    all_to_all x0 -> x2, starting transfers between devices: none -> 7.16 us  [gather_over(): blocks = lax.all_to_all(blocks, name, split_axis=0, concat_axis=0)]
    all_to_all x0 -> x2, waiting for transfers between devices: none -> 4.3 us  [gather_over(): blocks = lax.all_to_all(blocks, name, split_axis=0, concat_axis=0)]
    ppermute x12, starting transfers between devices: 22.1 us -> 18 us  [from_partner(): return lax.ppermute(value, axis, pairs)]
    another operation x0 -> x2, other arithmetic: none -> 3.46 us  [gather_over(): blocks = jnp.stack([x for _ in range(devices)])]
    reshape x6, local copies, waits for them, and re-layouts: 3.65 us -> 1.52 us  [bit_terms(): upper = current.reshape(shape)]
  transfers between devices with their start and end apart: 14 -> 14, of which waited for: 5 -> 4; matrix products, arithmetic and copies ran while one was open for 31% -> 31% of each run, Pallas kernels for 0% -> 0%
where the time goes in v1:
time: 184 us; the launch traced here: 182 us
  other arithmetic  61.3 us (33%)
  local copies, waits for them, and re-layouts  37.1 us (20%)
  matrix products  28.4 us (15%)
  starting transfers between devices  25.2 us (14%)
  between operations  16.5 us (9%)
  waiting for transfers between devices  13.8 us (8%)
    dot_general x4, matrix products, apply_blocks(): jnp.einsum('pcjt,cjts->pcs', chosen, blocks, precision=lax.Precision.HIGH...  28.4 us
    ppermute x12, starting transfers between devices, from_partner(): return lax.ppermute(value, axis, pairs)  18 us
    mul x12, other arithmetic, bit_terms(): repair[first + bit] * upper[:, 1]  15.6 us
    mul x12, other arithmetic, bit_terms(): fail[first + bit] * lower[:, 0]  14.9 us
    another operation x12, local copies, waits for them, and re-layouts, bit_terms(): lower = killed.reshape(shape)  10.3 us
    another operation x12, other arithmetic, bit_terms(): jnp.stack((repair[first + bit] * upper[:, 1], fail[first + bit] * lower[:...  9.64 us
    ppermute x12, waiting for transfers between devices, from_partner(): return lax.ppermute(value, axis, pairs)  9.53 us
    add x1, other arithmetic, local(): leaving + jnp.where(flag == 1, repair[low_count + bit], fail[low_count +...  7.44 us
  transfers between devices with their start and end apart: 14, of which 4 were waited for; matrix products, arithmetic and copies ran while one was open for 31% of the time, Pallas kernels for 0%

profile of v1, /device:TPU:0, one launch (start us, length us, event | category | flops | bytes accessed | tf_op | source)
XLA Modules:
  0.0 182.5 jit_solution(6956170318375877922)
XLA Ops:
  0.0 2.4 %pad_maximum_fusion = f32[2,64,2048]{2,1,0:T(8,128)} fusion(f32[1,64,2048]{2,1,0:T(8,128)} %bitcast.152), kind=kLoop, calls=%fused_computation.20 | loop fusion | flops 262144 | bytes 1572864 | tf_op jit(solution)/shard_map/stack | solution.py:11
  2.4 3.6 %all-to-all-start = ((f32[2,64,2048]{2,1,0:T(8,128)}), f32[2,64,2048]{2,1,0:T(8,128)S(1)}, u32[]{:S(2)}, u32[]{:S(2)}) async-start(f32[2,64,2048]{2,1,0:T(8,128)} %pad_maximum_fusion), calls=%async_computation | async-start | bytes 2097152 | tf_op jit(solution)/shard_map/all_to_all | solution.py:12
  26.2 1.3 slice_multiply_fusion.13
  27.6 1.4 slice_multiply_fusion.15
  29.6 1.3 slice_multiply_fusion.19
  30.9 1.6 slice_multiply_fusion.21
  33.1 7.4 %add_add_fusion = f32[64]{0:T(128)S(1)} fusion(f32[]{:T(128)S(6)} %select_n.398, f32[]{:T(128)S(6)} %select_n.397, f32[]{:T(128)S(6)} %select_n.396, f32[]{:T(128)S(6)} %select_n.395, f32[]{:T(128)S(6)} %select_n.394, f32[]{:T(128)S(6)} %select_n.393, f32[]{:T(128)} %bitcast.29, f32[]{:T(128)} %bitcast.27, f32[]{:T(128)} %bitcast.25, f32[]{:T(128)} %bitcast.23, ...), kind=kLoop, calls=%fused_computation.162 | loop fusion | flops 7296 | bytes 328 | tf_op jit(solution)/shard_map/add | solution.py:65
  40.6 1.6 slice_multiply_fusion.23
  42.9 1.8 %reshape_reshape.44 = f32[64,16,256]{2,1,0:T(8,128)} reshape(f32[64,2,2048]{2,1,0:T(2,128)S(1)} %copy.17) | data formatting | bytes 2097152 | tf_op jit(solution)/shard_map/reshape;reshape | solution.py:24
  44.8 1.8 %copy.19 = f32[64,16,256]{2,0,1:T(8,128)S(1)} copy(f32[64,16,256]{2,1,0:T(8,128)} %reshape_reshape.44) | data formatting | bytes 2097152 | tf_op jit(solution)/shard_map/reshape;reshape | solution.py:24
  46.6 1.8 %gather_fusion.3 = f32[24,64,256]{2,1,0:T(8,128)} fusion(f32[64,16,256]{2,0,1:T(8,128)S(1)} %copy.19, s32[1024]{0:T(1024)S(1)} %pad_clamp_fusion), kind=kCustom, calls=%fused_computation.1.clone | custom fusion | bytes 3145824 | tf_op jit(solution)/shard_map/jit(_take)/gather | solution.py:25
  48.4 7.3 %fusion.4 = f32[8,64,256,1]{2,1,3,0:T(8,128)S(1)} fusion(f32[8,3,256,256]{3,2,1,0:T(8,128)} %param.12, f32[8,3,64,256]{3,2,1,0:T(8,128)} %bitcast.159, pred[8,3]{1,0:T(8,128)(4,1)S(1)} %copy.21), kind=kOutput, calls=%fused_computation.10 | convolution fusion | flops 1208352768 | bytes 8388632 | tf_op jit(solution)/shard_map/pcjt,cjts->pcs/dot_general | solution.py:26
  56.9 0.9 reshape_reshape.49
  57.8 0.9 reshape_reshape.48
  58.7 1.0 reshape_reshape.47
  60.1 1.8 %gather_fusion.2 = f32[24,64,256]{2,1,0:T(8,128)} fusion(f32[64,16,256]{2,0,1:T(8,128)S(1)} %copy.19, s32[1024]{0:T(1024)S(1)} %pad_clamp_fusion.1), kind=kCustom, calls=%fused_computation.clone | custom fusion | bytes 3145824 | tf_op jit(solution)/shard_map/jit(_take)/gather | solution.py:25
  61.9 1.5 slice_multiply_fusion.12
  63.4 2.3 %slice_multiply_fusion.14 = f32[2,1,16,2048]{3,2,1,0:T(8,128)} fusion(f32[2,2,16,2048]{3,2,1,0:T(8,128)} %reshape_reshape.49, f32[]{:T(128)} %bitcast.25), kind=kLoop, calls=%fused_computation.82 | loop fusion | flops 65536 | bytes 524292 | tf_op jit(solution)/shard_map/mul | solution.py:44
  65.7 2.3 %slice_multiply_fusion.16 = f32[4,1,8,2048]{3,2,1,0:T(8,128)} fusion(f32[4,2,8,2048]{3,2,1,0:T(8,128)} %reshape_reshape.48, f32[]{:T(128)} %bitcast.21), kind=kLoop, calls=%fused_computation.84 | loop fusion | flops 65536 | bytes 524292 | tf_op jit(solution)/shard_map/mul | solution.py:44
  68.1 1.8 broadcast_select_fusion.11
  69.9 3.3 %collective-permute-start.5 = (f32[64,2048]{1,0:T(8,128)}, f32[64,2048]{1,0:T(8,128)}, u32[]{:S(2)}, u32[]{:S(2)}) collective-permute-start(f32[64,2048]{1,0:T(8,128)} %get-tuple-element.19), channel_id=1, source_target_pairs={{0,64},{2,66},{4,68},{6,70},{8,72},{10,74},{12,76},{14,78},{16,80}... | collective-permute-start | bytes 1572872 | tf_op jit(solution)/shard_map/ppermute | solution.py:19
  73.8 3.9 %collective-permute-start.3 = (f32[64,2048]{1,0:T(8,128)}, f32[64,2048]{1,0:T(8,128)}, u32[]{:S(2)}, u32[]{:S(2)}) collective-permute-start(f32[64,2048]{1,0:T(8,128)} %get-tuple-element.16), channel_id=1, source_target_pairs={{0,16},{2,18},{4,20},{6,22},{8,24},{10,26},{12,28},{14,30},{16,0},... | collective-permute-start | bytes 1572872 | tf_op jit(solution)/shard_map/ppermute | solution.py:19
  77.7 1.0 collective-permute-start.2
  78.7 3.0 %collective-permute-start.1 = (f32[64,2048]{1,0:T(8,128)}, f32[64,2048]{1,0:T(8,128)}, u32[]{:S(2)}, u32[]{:S(2)}) collective-permute-start(f32[64,2048]{1,0:T(8,128)} %get-tuple-element.18), channel_id=1, source_target_pairs={{0,4},{2,6},{4,0},{6,2},{8,12},{10,14},{12,8},{14,10},{16,20},{18,... | collective-permute-start | bytes 1572872 | tf_op jit(solution)/shard_map/ppermute | solution.py:19
  83.5 6.2 %fusion.12 = f32[8,8,8,256]{3,2,1,0:T(8,128)S(1)} fusion(f32[8,3,256,256]{3,2,1,0:T(8,128)} %param.10, f32[8,3,64,256]{3,2,1,0:T(8,128)S(1)} %bitcast.156, pred[8,3]{1,0:T(8,128)(4,1)S(1)} %copy.16), kind=kOutput, calls=%fused_computation.18 | convolution fusion | flops 1208352768 | bytes 8388632 | tf_op jit(solution)/shard_map/pcjt,cjts->pcs/dot_general | solution.py:26
  89.7 1.3 pad_maximum_fusion.2
  92.2 2.2 %pad_maximum_fusion.3 = f32[16,2,2,2048]{3,2,1,0:T(2,128)} fusion(f32[16,1,2,2048]{3,2,1,0:T(2,128)S(1)} %slice_multiply_fusion.20, f32[16,1,2,2048]{3,2,1,0:T(2,128)} %slice_multiply_fusion.21), kind=kLoop, calls=%fused_computation.31 | loop fusion | flops 131072 | bytes 1048576 | tf_op jit(solution)/shard_map/stack | solution.py:43
  95.0 2.3 %reshape.445 = f32[64,2048]{1,0:T(8,128)} reshape(f32[16,2,2,2048]{3,2,1,0:T(2,128)} %pad_maximum_fusion.3) | data formatting | bytes 1048576 | tf_op jit(solution)/shard_map/reshape | solution.py:46
  97.3 1.1 pad_maximum_fusion.6
  98.5 2.8 %collective-permute-done.2 = f32[64,2048]{1,0:T(8,128)} collective-permute-done((f32[64,2048]{1,0:T(8,128)}, f32[64,2048]{1,0:T(8,128)}, u32[]{:S(2)}, u32[]{:S(2)}) %collective-permute-start.2) | collective-permute-done | bytes 524320 | tf_op jit(solution)/shard_map/ppermute | solution.py:19
  101.4 2.5 %fusion.45 = f32[64,2048]{1,0:T(8,128)S(1)} fusion(f32[64,2048]{1,0:T(8,128)S(1)} %copy-done.2, f32[64,2048]{1,0:T(8,128)S(1)} %bitcast.167, f32[1,2,32,2048]{3,2,1,0:T(8,128)S(1)} %pad_maximum_fusion.7, f32[2,2,16,2048]{3,2,1,0:T(8,128)S(1)} %pad_maximum_fusion.6, f32[4,2,8,2048]{3,2,1,0:T(8,128)S(1)} %pad_maximum_fusion.5, ...), kind=kLoop, calls=%fused_computation.65 | loop fusion | flops 2883584 | bytes 7864604 | tf_op jit(solution)/shard_map/add | solution.py:81
  104.4 1.1 pad_maximum_fusion.1
  105.5 3.6 %all-to-all-start.1 = ((f32[2,64,2048]{2,1,0:T(8,128)}), f32[2,64,2048]{2,1,0:T(8,128)S(1)}, u32[]{:S(2)}, u32[]{:S(2)}) async-start(f32[2,64,2048]{2,1,0:T(8,128)} %pad_maximum_fusion.1), calls=%async_computation.1 | async-start | bytes 2097152 | tf_op jit(solution)/shard_map/all_to_all | solution.py:12
  109.1 1.3 slice_multiply_fusion.1
  110.4 1.4 slice_multiply_fusion.3
  112.4 1.4 slice_multiply_fusion.7
  113.8 1.5 slice_multiply_fusion.9
  115.6 1.6 slice_multiply_fusion.11
  117.2 4.3 %all-to-all-done.1 = f32[2,64,2048]{2,1,0:T(8,128)S(1)} async-done(((f32[2,64,2048]{2,1,0:T(8,128)}), f32[2,64,2048]{2,1,0:T(8,128)S(1)}, u32[]{:S(2)}, u32[]{:S(2)}) %all-to-all-start.1) | async-done | bytes 1048608 | tf_op jit(solution)/shard_map/all_to_all | solution.py:12
  122.3 1.8 %reshape_reshape.51 = f32[64,16,256]{2,1,0:T(8,128)} reshape(f32[64,2,2048]{2,1,0:T(2,128)S(1)} %copy.32) | data formatting | bytes 2097152 | tf_op jit(solution)/shard_map/reshape;reshape | solution.py:24
  124.1 1.8 %copy.34 = f32[64,16,256]{2,0,1:T(8,128)S(1)} copy(f32[64,16,256]{2,1,0:T(8,128)} %reshape_reshape.51) | data formatting | bytes 2097152 | tf_op jit(solution)/shard_map/reshape;reshape | solution.py:24
  125.9 1.8 %gather_fusion.4 = f32[24,64,256]{2,1,0:T(8,128)} fusion(f32[64,16,256]{2,0,1:T(8,128)S(1)} %copy.34, s32[1024]{0:T(1024)S(1)} %pad_clamp_fusion.1), kind=kCustom, calls=%fused_computation.2.clone | custom fusion | bytes 3145824 | tf_op jit(solution)/shard_map/jit(_take)/gather | solution.py:25
  127.8 1.8 gather_fusion.5
  129.6 7.3 %fusion = f32[8,64,256,1]{2,1,3,0:T(8,128)S(1)} fusion(f32[8,3,256,256]{3,2,1,0:T(8,128)} %param.12, f32[8,3,64,256]{3,2,1,0:T(8,128)} %bitcast.158, pred[8,3]{1,0:T(8,128)(4,1)S(1)} %copy.21), kind=kOutput, calls=%fused_computation.6 | convolution fusion | flops 1208352768 | bytes 8388632 | tf_op jit(solution)/shard_map/pcjt,cjts->pcs/dot_general | solution.py:26
  137.2 0.9 reshape_reshape.57
  139.0 0.9 reshape_reshape.55
  139.8 1.1 reshape_reshape.54
  140.9 1.1 reshape_reshape.52
  142.0 7.7 %fusion.15 = f32[8,8,8,256]{3,2,1,0:T(8,128)} fusion(f32[8,3,256,256]{3,2,1,0:T(8,128)} %param.10, f32[8,3,64,256]{3,2,1,0:T(8,128)S(1)} %bitcast.157, pred[8,3]{1,0:T(8,128)(4,1)S(1)} %copy.16), kind=kOutput, calls=%fused_computation.19 | convolution fusion | flops 1208352768 | bytes 8388632 | tf_op jit(solution)/shard_map/pcjt,cjts->pcs/dot_general | solution.py:26
  150.3 1.4 slice_multiply_fusion.2
  151.7 1.4 slice_multiply_fusion.4
  153.1 1.9 %broadcast_select_fusion.10 = (f32[64,2048]{1,0:T(8,128)}, f32[64,2048]{1,0:T(8,128)}, f32[64,2048]{1,0:T(8,128)}, f32[64,2048]{1,0:T(8,128)}, f32[64,2048]{1,0:T(8,128)}, /*index=5*/f32[64,2048]{1,0:T(8,128)}) fusion(f32[64,2048]{1,0:T(8,128)S(1)} %fusion.45, f32[64,2048]{1,0:T(8,128)S(1)} %bitcast.168, pred[]{:T(512)S(6)} %eq.116, pred[]{:T(512)S(6)} %eq.121, ...), kind=kLoop, calls=%fused_computation.102 | loop fusion | flops 786432 | bytes 4194310 | tf_op jit(solution)/shard_map/jit(_where)/select_n | solution.py:75
  155.0 1.8 %collective-permute-start.11 = (f32[64,2048]{1,0:T(8,128)}, f32[64,2048]{1,0:T(8,128)}, u32[]{:S(2)}, u32[]{:S(2)}) collective-permute-start(f32[64,2048]{1,0:T(8,128)} %get-tuple-element.9), channel_id=1, source_target_pairs={{0,64},{2,66},{4,68},{6,70},{8,72},{10,74},{12,76},{14,78},{16,80}... | collective-permute-start | bytes 1572872 | tf_op jit(solution)/shard_map/ppermute | solution.py:19
  156.9 1.2 collective-permute-start.9
  158.1 3.0 %collective-permute-start.7 = (f32[64,2048]{1,0:T(8,128)}, f32[64,2048]{1,0:T(8,128)}, u32[]{:S(2)}, u32[]{:S(2)}) collective-permute-start(f32[64,2048]{1,0:T(8,128)} %get-tuple-element.13), channel_id=1, source_target_pairs={{0,4},{2,6},{4,0},{6,2},{8,12},{10,14},{12,8},{14,10},{16,20},{18,... | collective-permute-start | bytes 1572872 | tf_op jit(solution)/shard_map/ppermute | solution.py:19
  163.3 1.1 reshape_reshape.53
  164.5 1.7 slice_multiply_fusion.8
  166.2 5.5 %collective-permute-done.11 = f32[64,2048]{1,0:T(8,128)} collective-permute-done((f32[64,2048]{1,0:T(8,128)}, f32[64,2048]{1,0:T(8,128)}, u32[]{:S(2)}, u32[]{:S(2)}) %collective-permute-start.11) | collective-permute-done | bytes 524320 | tf_op jit(solution)/shard_map/ppermute | solution.py:19
  171.7 2.1 %pad_maximum_fusion.9 = f32[16,2,2,2048]{3,2,1,0:T(2,128)} fusion(f32[16,1,2,2048]{3,2,1,0:T(2,128)S(1)} %slice_multiply_fusion.8, f32[16,1,2,2048]{3,2,1,0:T(2,128)} %slice_multiply_fusion.9), kind=kLoop, calls=%fused_computation.37 | loop fusion | flops 131072 | bytes 1048576 | tf_op jit(solution)/shard_map/stack | solution.py:43
  174.4 1.4 reshape.460
  175.8 1.1 pad_maximum_fusion.12
  176.9 1.0 pad_maximum_fusion.11
  177.9 1.1 collective-permute-done.8
  179.1 3.4 %fusion.35 = f32[64,2048]{1,0:T(8,128)} fusion(f32[64,2048]{1,0:T(8,128)S(1)} %fusion.45, f32[64,2048]{1,0:T(8,128)S(1)} %bitcast.166, f32[1,2,32,2048]{3,2,1,0:T(8,128)S(1)} %pad_maximum_fusion.13, f32[2,2,16,2048]{3,2,1,0:T(8,128)S(1)} %pad_maximum_fusion.12, f32[4,2,8,2048]{3,2,1,0:T(8,128)S(1)} %pad_maximum_fusion.11, ...), kind=kLoop, calls=%fused_computation.52 | loop fusion | flops 2883584 | bytes 7864604 | tf_op jit(solution)/shard_map/add | solution.py:81
  (117 shorter events, 19.0 us)
Async XLA Ops:
  0.0 7.0 %copy-start = (f32[8,2]{0,1:T(2,128)S(1)}, f32[8,2]{0,1:T(2,128)}, u32[]{:S(2)}) copy-start(f32[8,2]{0,1:T(2,128)} %param.15) | copy-start | bytes 196
  0.0 6.0 %copy-start.21 = (s32[8,3]{0,1:T(4,128)S(1)}, s32[8,3]{0,1:T(4,128)}, u32[]{:S(2)}) copy-start(s32[8,3]{0,1:T(4,128)} %param.11) | copy-start | bytes 292
  0.0 6.0 %copy-start.22 = (s32[8,3]{0,1:T(4,128)S(1)}, s32[8,3]{0,1:T(4,128)}, u32[]{:S(2)}) copy-start(s32[8,3]{0,1:T(4,128)} %param.13) | copy-start | bytes 292
  0.0 6.1 %copy-start.2 = (f32[64,2048]{1,0:T(8,128)S(1)}, f32[64,2048]{1,0:T(8,128)}, u32[]{:S(2)}) copy-start(f32[64,2048]{1,0:T(8,128)} %param.9) | copy-start | bytes 1572868
  2.4 39.8 %all-to-all-start = ((f32[2,64,2048]{2,1,0:T(8,128)}), f32[2,64,2048]{2,1,0:T(8,128)S(1)}, u32[]{:S(2)}, u32[]{:S(2)}) async-start(f32[2,64,2048]{2,1,0:T(8,128)} %pad_maximum_fusion), calls=%async_computation | async-start | bytes 2097152 | tf_op jit(solution)/shard_map/all_to_all | solution.py:12
  6.2 0.8 copy-start.23
  68.1 13.7 %copy-start.10 = (f32[8,2,4,2048]{3,2,1,0:T(4,128)S(1)}, f32[8,2,4,2048]{3,2,1,0:T(4,128)}, u32[]{:S(2)}) copy-start(f32[8,2,4,2048]{3,2,1,0:T(4,128)} %reshape_reshape.47) | copy-start | bytes 1572868
  68.1 15.2 %copy-start.17 = (f32[1,1,32,2048]{3,2,1,0:T(8,128)S(1)}, f32[1,1,32,2048]{3,2,1,0:T(8,128)}, u32[]{:S(2)}) copy-start(f32[1,1,32,2048]{3,2,1,0:T(8,128)} %slice_multiply_fusion.13) | copy-start | bytes 786436
  69.9 13.5 %copy-start.18 = (f32[8,1,4,2048]{3,2,1,0:T(4,128)S(1)}, f32[8,1,4,2048]{3,2,1,0:T(4,128)}, u32[]{:S(2)}) copy-start(f32[8,1,4,2048]{3,2,1,0:T(4,128)} %slice_multiply_fusion.19) | copy-start | bytes 786436
  69.9 22.3 %collective-permute-start.5 = (f32[64,2048]{1,0:T(8,128)}, f32[64,2048]{1,0:T(8,128)}, u32[]{:S(2)}, u32[]{:S(2)}) collective-permute-start(f32[64,2048]{1,0:T(8,128)} %get-tuple-element.19), channel_id=1, source_target_pairs={{0,64},{2,66},{4,68},{6,70},{8,72},{10,74},{12,76},{14,78},{16,80}... | collective-permute-start | bytes 1572872 | tf_op jit(solution)/shard_map/ppermute | solution.py:19
  73.2 25.3 %collective-permute-start.4 = (f32[64,2048]{1,0:T(8,128)}, f32[64,2048]{1,0:T(8,128)}, u32[]{:S(2)}, u32[]{:S(2)}) collective-permute-start(f32[64,2048]{1,0:T(8,128)} %get-tuple-element.15), channel_id=1, source_target_pairs={{0,32},{2,34},{4,36},{6,38},{8,40},{10,42},{12,44},{14,46},{16,48}... | collective-permute-start | bytes 1572872 | tf_op jit(solution)/shard_map/ppermute | solution.py:19
  73.8 24.7 %collective-permute-start.3 = (f32[64,2048]{1,0:T(8,128)}, f32[64,2048]{1,0:T(8,128)}, u32[]{:S(2)}, u32[]{:S(2)}) collective-permute-start(f32[64,2048]{1,0:T(8,128)} %get-tuple-element.16), channel_id=1, source_target_pairs={{0,16},{2,18},{4,20},{6,22},{8,24},{10,26},{12,28},{14,30},{16,0},... | collective-permute-start | bytes 1572872 | tf_op jit(solution)/shard_map/ppermute | solution.py:19
  77.7 23.7 %collective-permute-start.2 = (f32[64,2048]{1,0:T(8,128)}, f32[64,2048]{1,0:T(8,128)}, u32[]{:S(2)}, u32[]{:S(2)}) collective-permute-start(f32[64,2048]{1,0:T(8,128)} %get-tuple-element.17), channel_id=1, source_target_pairs={{0,8},{2,10},{4,12},{6,14},{8,0},{10,2},{12,4},{14,6},{16,24},{18,... | collective-permute-start | bytes 1572872 | tf_op jit(solution)/shard_map/ppermute | solution.py:19
  78.7 4.7 %copy-start.3 = (f32[24,64,256]{2,1,0:T(8,128)S(1)}, f32[24,64,256]{2,1,0:T(8,128)}, u32[]{:S(2)}) copy-start(f32[24,64,256]{2,1,0:T(8,128)} %gather_fusion.2) | copy-start | bytes 4718596
  78.7 22.6 %collective-permute-start.1 = (f32[64,2048]{1,0:T(8,128)}, f32[64,2048]{1,0:T(8,128)}, u32[]{:S(2)}, u32[]{:S(2)}) collective-permute-start(f32[64,2048]{1,0:T(8,128)} %get-tuple-element.18), channel_id=1, source_target_pairs={{0,4},{2,6},{4,0},{6,2},{8,12},{10,14},{12,8},{14,10},{16,20},{18,... | collective-permute-start | bytes 1572872 | tf_op jit(solution)/shard_map/ppermute | solution.py:19
  83.5 6.2 %copy-start.20 = (f32[32,1,1,2048]{3,1,0,2:T(1,128)S(1)}, f32[32,1,1,2048]{3,1,0,2:T(1,128)}, u32[]{:S(2)}) copy-start(f32[32,1,1,2048]{3,1,0,2:T(1,128)} %slice_multiply_fusion.23) | copy-start | bytes 786436
  92.1 2.5 %copy-start.7 = (f32[32,2,1,2048]{3,1,0,2:T(2,128)S(1)}, f32[32,2,1,2048]{3,1,0,2:T(2,128)}, u32[]{:S(2)}) copy-start(f32[32,2,1,2048]{3,1,0,2:T(2,128)} %pad_maximum_fusion.2) | copy-start | bytes 1572868
  92.2 9.2 %collective-permute-start = (f32[64,2048]{1,0:T(8,128)}, f32[64,2048]{1,0:T(8,128)}, u32[]{:S(2)}, u32[]{:S(2)}) collective-permute-start(f32[64,2048]{1,0:T(8,128)} %get-tuple-element.14), channel_id=1, source_target_pairs={{0,2},{2,0},{4,6},{6,4},{8,10},{10,8},{12,14},{14,12},{16,18},{18,... | collective-permute-start | bytes 1572872 | tf_op jit(solution)/shard_map/ppermute | solution.py:19
  95.0 3.4 %copy-start.19 = (f32[4,1,8,2048]{3,2,1,0:T(8,128)S(1)}, f32[4,1,8,2048]{3,2,1,0:T(8,128)}, u32[]{:S(2)}) copy-start(f32[4,1,8,2048]{3,2,1,0:T(8,128)} %slice_multiply_fusion.16) | copy-start | bytes 786436
  97.3 4.1 %copy-start.6 = (f32[64,2048]{1,0:T(8,128)S(1)}, f32[64,2048]{1,0:T(8,128)}, u32[]{:S(2)}) copy-start(f32[64,2048]{1,0:T(8,128)} %reshape.445) | copy-start | bytes 1572868
  105.5 16.0 %all-to-all-start.1 = ((f32[2,64,2048]{2,1,0:T(8,128)}), f32[2,64,2048]{2,1,0:T(8,128)S(1)}, u32[]{:S(2)}, u32[]{:S(2)}) async-start(f32[2,64,2048]{2,1,0:T(8,128)} %pad_maximum_fusion.1), calls=%async_computation.1 | async-start | bytes 2097152 | tf_op jit(solution)/shard_map/all_to_all | solution.py:12
  139.0 3.1 %copy-start.4 = (f32[24,64,256]{2,1,0:T(8,128)S(1)}, f32[24,64,256]{2,1,0:T(8,128)}, u32[]{:S(2)}) copy-start(f32[24,64,256]{2,1,0:T(8,128)} %gather_fusion.4) | copy-start | bytes 4718596
  142.0 7.7 %copy-start.13 = (f32[1,2,32,2048]{3,2,1,0:T(8,128)S(1)}, f32[1,2,32,2048]{3,2,1,0:T(8,128)}, u32[]{:S(2)}) copy-start(f32[1,2,32,2048]{3,2,1,0:T(8,128)} %reshape_reshape.57) | copy-start | bytes 1572868
  142.0 8.3 %copy-start.12 = (f32[2,2,16,2048]{3,2,1,0:T(8,128)S(1)}, f32[2,2,16,2048]{3,2,1,0:T(8,128)}, u32[]{:S(2)}) copy-start(f32[2,2,16,2048]{3,2,1,0:T(8,128)} %reshape_reshape.56) | copy-start | bytes 1572868
  142.0 9.7 %copy-start.11 = (f32[4,2,8,2048]{3,2,1,0:T(8,128)S(1)}, f32[4,2,8,2048]{3,2,1,0:T(8,128)}, u32[]{:S(2)}) copy-start(f32[4,2,8,2048]{3,2,1,0:T(8,128)} %reshape_reshape.55) | copy-start | bytes 1572868
  153.1 8.0 %copy-start.9 = (f32[8,2,4,2048]{3,2,1,0:T(4,128)S(1)}, f32[8,2,4,2048]{3,2,1,0:T(4,128)}, u32[]{:S(2)}) copy-start(f32[8,2,4,2048]{3,2,1,0:T(4,128)} %reshape_reshape.54) | copy-start | bytes 1572868
  153.1 8.7 %copy-start.8 = (f32[32,2,1,2048]{3,1,0,2:T(2,128)S(1)}, f32[32,2,1,2048]{3,1,0,2:T(2,128)}, u32[]{:S(2)}) copy-start(f32[32,2,1,2048]{3,1,0,2:T(2,128)} %reshape_reshape.52) | copy-start | bytes 1572868
  153.1 9.5 %copy-start.14 = (f32[1,1,32,2048]{3,2,1,0:T(8,128)S(1)}, f32[1,1,32,2048]{3,2,1,0:T(8,128)}, u32[]{:S(2)}) copy-start(f32[1,1,32,2048]{3,2,1,0:T(8,128)} %slice_multiply_fusion.1) | copy-start | bytes 786436
  155.0 7.6 %copy-start.15 = (f32[8,1,4,2048]{3,2,1,0:T(4,128)S(1)}, f32[8,1,4,2048]{3,2,1,0:T(4,128)}, u32[]{:S(2)}) copy-start(f32[8,1,4,2048]{3,2,1,0:T(4,128)} %slice_multiply_fusion.7) | copy-start | bytes 786436
  155.0 16.7 %collective-permute-start.11 = (f32[64,2048]{1,0:T(8,128)}, f32[64,2048]{1,0:T(8,128)}, u32[]{:S(2)}, u32[]{:S(2)}) collective-permute-start(f32[64,2048]{1,0:T(8,128)} %get-tuple-element.9), channel_id=1, source_target_pairs={{0,64},{2,66},{4,68},{6,70},{8,72},{10,74},{12,76},{14,78},{16,80}... | collective-permute-start | bytes 1572872 | tf_op jit(solution)/shard_map/ppermute | solution.py:19
  156.9 21.0 %collective-permute-start.10 = (f32[64,2048]{1,0:T(8,128)}, f32[64,2048]{1,0:T(8,128)}, u32[]{:S(2)}, u32[]{:S(2)}) collective-permute-start(f32[64,2048]{1,0:T(8,128)} %get-tuple-element.10), channel_id=1, source_target_pairs={{0,32},{2,34},{4,36},{6,38},{8,40},{10,42},{12,44},{14,46},{16,48}... | collective-permute-start | bytes 1572872 | tf_op jit(solution)/shard_map/ppermute | solution.py:19
  156.9 21.0 %collective-permute-start.9 = (f32[64,2048]{1,0:T(8,128)}, f32[64,2048]{1,0:T(8,128)}, u32[]{:S(2)}, u32[]{:S(2)}) collective-permute-start(f32[64,2048]{1,0:T(8,128)} %get-tuple-element.11), channel_id=1, source_target_pairs={{0,16},{2,18},{4,20},{6,22},{8,24},{10,26},{12,28},{14,30},{16,0},... | collective-permute-start | bytes 1572872 | tf_op jit(solution)/shard_map/ppermute | solution.py:19
  158.0 21.0 %collective-permute-start.8 = (f32[64,2048]{1,0:T(8,128)}, f32[64,2048]{1,0:T(8,128)}, u32[]{:S(2)}, u32[]{:S(2)}) collective-permute-start(f32[64,2048]{1,0:T(8,128)} %get-tuple-element.12), channel_id=1, source_target_pairs={{0,8},{2,10},{4,12},{6,14},{8,0},{10,2},{12,4},{14,6},{16,24},{18,... | collective-permute-start | bytes 1572872 | tf_op jit(solution)/shard_map/ppermute | solution.py:19
  158.1 4.8 %copy-start.16 = (f32[32,1,1,2048]{3,1,0,2:T(1,128)S(1)}, f32[32,1,1,2048]{3,1,0,2:T(1,128)}, u32[]{:S(2)}) copy-start(f32[32,1,1,2048]{3,1,0,2:T(1,128)} %slice_multiply_fusion.11) | copy-start | bytes 786436
  158.1 21.0 %collective-permute-start.7 = (f32[64,2048]{1,0:T(8,128)}, f32[64,2048]{1,0:T(8,128)}, u32[]{:S(2)}, u32[]{:S(2)}) collective-permute-start(f32[64,2048]{1,0:T(8,128)} %get-tuple-element.13), channel_id=1, source_target_pairs={{0,4},{2,6},{4,0},{6,2},{8,12},{10,14},{12,8},{14,10},{16,20},{18,... | collective-permute-start | bytes 1572872 | tf_op jit(solution)/shard_map/ppermute | solution.py:19
  163.3 10.5 %copy-start.5 = (f32[8,8,8,256]{3,2,1,0:T(8,128)S(1)}, f32[8,8,8,256]{3,2,1,0:T(8,128)}, u32[]{:S(2)}) copy-start(f32[8,8,8,256]{3,2,1,0:T(8,128)} %fusion.15) | copy-start | bytes 1572868
  171.7 7.4 %collective-permute-start.6 = (f32[64,2048]{1,0:T(8,128)}, f32[64,2048]{1,0:T(8,128)}, u32[]{:S(2)}, u32[]{:S(2)}) collective-permute-start(f32[64,2048]{1,0:T(8,128)} %get-tuple-element.8), channel_id=1, source_target_pairs={{0,2},{2,0},{4,6},{6,4},{8,10},{10,8},{12,14},{14,12},{16,18},{18,... | collective-permute-start | bytes 1572872 | tf_op jit(solution)/shard_map/ppermute | solution.py:19
  179.1 3.4 %copy-start.1 = (f32[8,2]{0,1:T(2,128)S(1)}, f32[8,2]{0,1:T(2,128)}, u32[]{:S(2)}) copy-start(f32[8,2]{0,1:T(2,128)} %param.15) | copy-start | bytes 196
